TPU v7x, 128 devices: a whole 4x4x4 slice. The times are simulated.
128 devices in a mesh: row: 16 (over x, z), col: 8 (over y, core).
Axes of the slice: x: 4, y: 4, z: 4, core: 2. Of those that a mesh axis runs over, the one named last changes fastest.
Arguments:
- t_upper: bfloat16 [3, 4096, 4096], P(None, 'row', 'col'), may hold values from -0.03125 to 0.03125
- t_old: bfloat16 [3, 4096, 24576], P(None, 'row', 'col'), may hold values from -0.03125 to 0.03125
- inverses: bfloat16 [3, 4096, 4096], P(None, 'row', 'col'), may hold values from -1 to 1.5, as said below
- forcing: float32 [3, 4096, 128], P(None, 'row'), may hold values from -6 to 6
- x_old: bfloat16 [24576, 128], P('col'), may hold values from -6 to 6
- offsets: float32 [128], replicated, may hold values from -0.5 to 0.5
- starts: int32 [128], replicated, may hold values from 0 to 36864
- column_map: int32 [128], replicated, may hold values from 0 to 127, each once
- z_cols: bfloat16 [49152, 3, 4096], P('row', None, 'col'), may hold values from -0.0546875 to 0.0546875
- acc: float32 [49152, 128], P(('row', 'col')), may hold values from -6 to 6
Outputs:
- solved: float32 [3, 4096, 128], P(None, ('row', 'col'))
- acc_out: float32 [49152, 128], P(('row', 'col'))
Inputs may be any that keep to these rules, and one draw needn't show every extreme that they name: `inverses`: dense matrices with a dominant positive diagonal.
All inputs are finite; a program needn't handle non-finite values.
Results may differ from a plain program's by a relative error of at most 0.0003.
Values may be sent and summed in bfloat16 or wider, within the bound.
No kernel may reach another device: no remote copies, remote signals or barrier semaphores. Data moves between devices by JAX's collectives and lax.ppermute only.
A program may use at most 128 MiB of HBM per device.

v0:
```python
import jax
import jax.numpy as jnp
from jax import lax
from jax.sharding import PartitionSpec as P

NEUMANN = 3


def split_pair(values):
    upper = values.astype(jnp.bfloat16)
    lower = (values - lax.optimization_barrier(upper).astype(jnp.float32)).astype(jnp.bfloat16)
    return jnp.concatenate([upper, lower], axis=-1)


def body(t_upper, t_old, inverses, forcing, x_old, offsets, starts, column_map, z_cols, acc):
    n_col = lax.axis_size("col")
    row_idx = lax.axis_index("row")
    col_idx = lax.axis_index("col")
    steps = forcing.shape[0]
    row_block = t_upper.shape[1]
    col_block = t_upper.shape[2]
    width = forcing.shape[2]
    old_cols = x_old.shape[0]
    full_rows = col_block * n_col
    share = row_block // n_col
    pairs = {}
    count = 0
    for first in range(steps):
        for second in range(first + 1, steps):
            pairs[first, second] = count
            count = count + 1

    def fold_pair(product):
        return product[:, :width] + product[:, width:]

    old_rows = steps * full_rows + col_idx * old_cols + jnp.arange(old_cols, dtype=jnp.int32)
    old_live = old_rows[:, None] < starts[None, :]
    old_vals = jnp.where(old_live, x_old, jnp.zeros_like(x_old))
    local_start = row_idx * row_block

    def reduce_rows(partial_value):
        return lax.psum(partial_value, "col")

    def spread_rows(values):
        return lax.all_gather(values, "row", axis=0, tiled=True)

    def own_cols(whole):
        return lax.dynamic_slice_in_dim(whole, col_idx * col_block, col_block, 0)

    solved_full = {}
    pieces = {}
    for step in reversed(range(steps)):
        partial_value = -jnp.dot(t_old[step], old_vals, preferred_element_type=jnp.float32)
        for later in range(step + 1, steps):
            partial_value = partial_value - fold_pair(
                jnp.dot(
                    t_upper[pairs[step, later]],
                    own_cols(solved_full[later]),
                    preferred_element_type=jnp.float32,
                )
            )
        rhs = reduce_rows(partial_value) + forcing[step]
        gathered = spread_rows(split_pair(rhs))
        term = reduce_rows(
            fold_pair(
                jnp.dot(inverses[step], own_cols(gathered), preferred_element_type=jnp.float32)
            )
        )
        total = term
        for extra in range(1, NEUMANN):
            gathered = spread_rows(split_pair(term))
            term = (
                reduce_rows(
                    fold_pair(
                        jnp.dot(
                            inverses[step], own_cols(gathered), preferred_element_type=jnp.float32
                        )
                    )
                )
                * offsets[None, :]
            )
            total = total + term
        rows = step * full_rows + local_start + jnp.arange(row_block, dtype=jnp.int32)
        total = jnp.where(rows[:, None] < starts[None, :], total, jnp.zeros_like(total))
        pieces[step] = lax.dynamic_slice_in_dim(total, col_idx * share, share, 0)
        solved_full[step] = spread_rows(split_pair(total))
    stacked = jnp.concatenate([own_cols(solved_full[step]) for step in range(steps)], axis=0)
    one_hot = (jnp.arange(width, dtype=jnp.int32)[:, None] == column_map[None, :]).astype(
        jnp.bfloat16
    )
    picked_upper = jnp.dot(stacked[:, :width], one_hot, preferred_element_type=jnp.float32).astype(
        jnp.bfloat16
    )
    picked_lower = jnp.dot(stacked[:, width:], one_hot, preferred_element_type=jnp.float32).astype(
        jnp.bfloat16
    )
    picked = jnp.concatenate([picked_upper, picked_lower], axis=1)
    z_rows = z_cols.shape[0]
    z_flat = z_cols.reshape(z_rows, steps * col_block)
    contribution = lax.psum_scatter(
        fold_pair(jnp.dot(z_flat, picked, preferred_element_type=jnp.float32)),
        "col",
        scatter_dimension=0,
        tiled=True,
    )
    solved = jnp.stack([pieces[step] for step in range(steps)])
    return (solved, acc + contribution)


def solution(mesh):
    placed = (
        P(None, "row", "col"),
        P(None, "row", "col"),
        P(None, "row", "col"),
        P(None, "row", None),
        P("col", None),
        P(),
        P(),
        P(),
        P("row", None, "col"),
        P(("row", "col"), None),
    )
    return jax.shard_map(
        body,
        mesh=mesh,
        in_specs=placed,
        out_specs=(P(None, ("row", "col"), None), P(("row", "col"), None)),
        check_vma=False,
    )
```

profile of v0, /device:TPU:0, one launch (start us, length us, event | category | flops | bytes accessed | tf_op | source)
XLA Modules:
  0.0 1396.4 jit_solution(2241294068387488249)
XLA Ops:
  11.0 62.4 %all-reduce.13.cloned.1.call-done = f32[256,128]{0,1:T(8,128)} async-done(((f32[256,128]{0,1:T(8,128)}), f32[256,128]{0,1:T(8,128)}) %all-reduce.13.cloned.1.call-update) | async-done | bytes 131088 | tf_op jit(solution)/shard_map/psum | solution.py:42
  76.0 46.2 %all-gather.13.cloned.1.call-done = bf16[4096,256]{0,1:T(8,128)(2,1)} async-done(((bf16[256,256]{0,1:T(8,128)(2,1)}), bf16[4096,256]{0,1:T(8,128)(2,1)}) %all-gather.13.cloned.1.call-update) | async-done | bytes 2097168 | tf_op jit(solution)/shard_map/all_gather | solution.py:45
  124.2 60.2 %all-reduce.15.cloned.1.call-done = f32[256,128]{0,1:T(8,128)} async-done(((f32[256,128]{0,1:T(8,128)}), f32[256,128]{0,1:T(8,128)}) %all-reduce.15.cloned.1.call-update) | async-done | bytes 131088 | tf_op jit(solution)/shard_map/psum | solution.py:42
  187.0 46.2 %all-gather.15.cloned.1.call-done = bf16[4096,256]{0,1:T(8,128)(2,1)} async-done(((bf16[256,256]{0,1:T(8,128)(2,1)}), bf16[4096,256]{0,1:T(8,128)(2,1)}) %all-gather.15.cloned.1.call-update) | async-done | bytes 2097168 | tf_op jit(solution)/shard_map/all_gather | solution.py:45
  235.2 60.1 %all-reduce.17.cloned.1.call-done = f32[256,128]{0,1:T(8,128)} async-done(((f32[256,128]{0,1:T(8,128)}), f32[256,128]{0,1:T(8,128)}) %all-reduce.17.cloned.1.call-update) | async-done | bytes 131088 | tf_op jit(solution)/shard_map/psum | solution.py:42
  298.1 46.2 %all-gather.17.cloned.1.call-done = bf16[4096,256]{0,1:T(8,128)(2,1)} async-done(((bf16[256,256]{0,1:T(8,128)(2,1)}), bf16[4096,256]{0,1:T(8,128)(2,1)}) %all-gather.17.cloned.1.call-update) | async-done | bytes 2097168 | tf_op jit(solution)/shard_map/all_gather | solution.py:45
  346.3 60.2 %all-reduce.19.cloned.1.call-done = f32[256,128]{0,1:T(8,128)} async-done(((f32[256,128]{0,1:T(8,128)}), f32[256,128]{0,1:T(8,128)}) %all-reduce.19.cloned.1.call-update) | async-done | bytes 131088 | tf_op jit(solution)/shard_map/psum | solution.py:42
  408.3 47.0 %all-gather.19.cloned.1.call-done = bf16[4096,256]{0,1:T(8,128)(2,1)} async-done(((bf16[256,256]{0,1:T(8,128)(2,1)}), bf16[4096,256]{0,1:T(8,128)(2,1)}) %all-gather.19.cloned.1.call-update) | async-done | bytes 2097168 | tf_op jit(solution)/shard_map/all_gather | solution.py:45
  460.3 59.3 %all-reduce.21.cloned.1.call-done = f32[256,128]{0,1:T(8,128)} async-done(((f32[256,128]{0,1:T(8,128)}), f32[256,128]{0,1:T(8,128)}) %all-reduce.21.cloned.1.call-update) | async-done | bytes 131088 | tf_op jit(solution)/shard_map/psum | solution.py:42
  522.1 46.2 %all-gather.21.cloned.1.call-done = bf16[4096,256]{0,1:T(8,128)(2,1)} async-done(((bf16[256,256]{0,1:T(8,128)(2,1)}), bf16[4096,256]{0,1:T(8,128)(2,1)}) %all-gather.21.cloned.1.call-update) | async-done | bytes 2097168 | tf_op jit(solution)/shard_map/all_gather | solution.py:45
  570.3 60.2 %all-reduce.23.cloned.1.call-done = f32[256,128]{0,1:T(8,128)} async-done(((f32[256,128]{0,1:T(8,128)}), f32[256,128]{0,1:T(8,128)}) %all-reduce.23.cloned.1.call-update) | async-done | bytes 131088 | tf_op jit(solution)/shard_map/psum | solution.py:42
  633.2 46.2 %all-gather.23.cloned.1.call-done = bf16[4096,256]{0,1:T(8,128)(2,1)} async-done(((bf16[256,256]{0,1:T(8,128)(2,1)}), bf16[4096,256]{0,1:T(8,128)(2,1)}) %all-gather.23.cloned.1.call-update) | async-done | bytes 2097168 | tf_op jit(solution)/shard_map/all_gather | solution.py:45
  681.4 60.2 %all-reduce.25.cloned.1.call-done = f32[256,128]{0,1:T(8,128)} async-done(((f32[256,128]{0,1:T(8,128)}), f32[256,128]{0,1:T(8,128)}) %all-reduce.25.cloned.1.call-update) | async-done | bytes 131088 | tf_op jit(solution)/shard_map/psum | solution.py:42
  744.4 46.2 %all-gather.25.cloned.1.call-done = bf16[4096,256]{0,1:T(8,128)(2,1)} async-done(((bf16[256,256]{0,1:T(8,128)(2,1)}), bf16[4096,256]{0,1:T(8,128)(2,1)}) %all-gather.25.cloned.1.call-update) | async-done | bytes 2097168 | tf_op jit(solution)/shard_map/all_gather | solution.py:45
  792.6 60.1 %all-reduce.27.cloned.1.call-done = f32[256,128]{0,1:T(8,128)} async-done(((f32[256,128]{0,1:T(8,128)}), f32[256,128]{0,1:T(8,128)}) %all-reduce.27.cloned.1.call-update) | async-done | bytes 131088 | tf_op jit(solution)/shard_map/psum | solution.py:42
  854.7 46.6 %all-gather.27.cloned.1.call-done = bf16[4096,256]{0,1:T(8,128)(2,1)} async-done(((bf16[256,256]{0,1:T(8,128)(2,1)}), bf16[4096,256]{0,1:T(8,128)(2,1)}) %all-gather.27.cloned.1.call-update) | async-done | bytes 2097168 | tf_op jit(solution)/shard_map/all_gather | solution.py:45
  906.3 59.3 %all-reduce.29.cloned.1.call-done = f32[256,128]{0,1:T(8,128)} async-done(((f32[256,128]{0,1:T(8,128)}), f32[256,128]{0,1:T(8,128)}) %all-reduce.29.cloned.1.call-update) | async-done | bytes 131088 | tf_op jit(solution)/shard_map/psum | solution.py:42
  968.1 46.2 %all-gather.29.cloned.1.call-done = bf16[4096,256]{0,1:T(8,128)(2,1)} async-done(((bf16[256,256]{0,1:T(8,128)(2,1)}), bf16[4096,256]{0,1:T(8,128)(2,1)}) %all-gather.29.cloned.1.call-update) | async-done | bytes 2097168 | tf_op jit(solution)/shard_map/all_gather | solution.py:45
  1016.3 60.2 %all-reduce.31.cloned.1.call-done = f32[256,128]{0,1:T(8,128)} async-done(((f32[256,128]{0,1:T(8,128)}), f32[256,128]{0,1:T(8,128)}) %all-reduce.31.cloned.1.call-update) | async-done | bytes 131088 | tf_op jit(solution)/shard_map/psum | solution.py:42
  1079.2 46.2 %all-gather.31.cloned.1.call-done = bf16[4096,256]{0,1:T(8,128)(2,1)} async-done(((bf16[256,256]{0,1:T(8,128)(2,1)}), bf16[4096,256]{0,1:T(8,128)(2,1)}) %all-gather.31.cloned.1.call-update) | async-done | bytes 2097168 | tf_op jit(solution)/shard_map/all_gather | solution.py:45
  1127.3 60.2 %all-reduce.33.cloned.1.call-done = f32[256,128]{0,1:T(8,128)} async-done(((f32[256,128]{0,1:T(8,128)}), f32[256,128]{0,1:T(8,128)}) %all-reduce.33.cloned.1.call-update) | async-done | bytes 131088 | tf_op jit(solution)/shard_map/psum | solution.py:42
  1190.4 46.2 %all-gather.33.cloned.1.call-done = bf16[4096,256]{0,1:T(8,128)(2,1)} async-done(((bf16[256,256]{0,1:T(8,128)(2,1)}), bf16[4096,256]{0,1:T(8,128)(2,1)}) %all-gather.33.cloned.1.call-update) | async-done | bytes 2097168 | tf_op jit(solution)/shard_map/all_gather | solution.py:45
  1238.6 60.2 %all-reduce.35.cloned.1.call-done = f32[256,128]{0,1:T(8,128)} async-done(((f32[256,128]{0,1:T(8,128)}), f32[256,128]{0,1:T(8,128)}) %all-reduce.35.cloned.1.call-update) | async-done | bytes 131088 | tf_op jit(solution)/shard_map/psum | solution.py:42
  1313.2 34.3 %all-gather.35.cloned.1.call-done = bf16[4096,256]{0,1:T(8,128)(2,1)} async-done(((bf16[256,256]{0,1:T(8,128)(2,1)}), bf16[4096,256]{0,1:T(8,128)(2,1)}) %all-gather.35.cloned.1.call-update) | async-done | bytes 2097168 | tf_op jit(solution)/shard_map/all_gather | solution.py:45
  (164 shorter events, 115.4 us)
Async XLA Ops:
  10.8 111.4 %all-gather.13.cloned.1.call-start = ((), (), s32[]{:S(2)}) async-start(), calls=%async_computation.2 | async-start | bytes 2228224 | tf_op jit(solution)/shard_map/all_gather | solution.py:45
  75.9 108.5 %all-reduce.15.cloned.1.call-start = ((), (), s32[]{:S(2)}) async-start(), calls=%async_computation.3 | async-start | bytes 262144 | tf_op jit(solution)/shard_map/psum | solution.py:42
  124.1 109.1 %all-gather.15.cloned.1.call-start = ((), (), s32[]{:S(2)}) async-start(), calls=%async_computation.4 | async-start | bytes 2228224 | tf_op jit(solution)/shard_map/all_gather | solution.py:45
  187.0 108.3 %all-reduce.17.cloned.1.call-start = ((), (), s32[]{:S(2)}) async-start(), calls=%async_computation.5 | async-start | bytes 262144 | tf_op jit(solution)/shard_map/psum | solution.py:42
  235.2 109.1 %all-gather.17.cloned.1.call-start = ((), (), s32[]{:S(2)}) async-start(), calls=%async_computation.6 | async-start | bytes 2228224 | tf_op jit(solution)/shard_map/all_gather | solution.py:45
  298.1 108.4 %all-reduce.19.cloned.1.call-start = ((), (), s32[]{:S(2)}) async-start(), calls=%async_computation.7 | async-start | bytes 262144 | tf_op jit(solution)/shard_map/psum | solution.py:42
  346.2 109.1 %all-gather.19.cloned.1.call-start = ((), (), s32[]{:S(2)}) async-start(), calls=%async_computation.8 | async-start | bytes 2228224 | tf_op jit(solution)/shard_map/all_gather | solution.py:45
  408.2 111.3 %all-reduce.21.cloned.1.call-start = ((), (), s32[]{:S(2)}) async-start(), calls=%async_computation.9 | async-start | bytes 262144 | tf_op jit(solution)/shard_map/psum | solution.py:42
  460.1 108.2 %all-gather.21.cloned.1.call-start = ((), (), s32[]{:S(2)}) async-start(), calls=%async_computation.10 | async-start | bytes 2228224 | tf_op jit(solution)/shard_map/all_gather | solution.py:45
  522.1 108.5 %all-reduce.23.cloned.1.call-start = ((), (), s32[]{:S(2)}) async-start(), calls=%async_computation.11 | async-start | bytes 262144 | tf_op jit(solution)/shard_map/psum | solution.py:42
  570.3 109.1 %all-gather.23.cloned.1.call-start = ((), (), s32[]{:S(2)}) async-start(), calls=%async_computation.12 | async-start | bytes 2228224 | tf_op jit(solution)/shard_map/all_gather | solution.py:45
  633.1 108.4 %all-reduce.25.cloned.1.call-start = ((), (), s32[]{:S(2)}) async-start(), calls=%async_computation.13 | async-start | bytes 262144 | tf_op jit(solution)/shard_map/psum | solution.py:42
  681.3 109.3 %all-gather.25.cloned.1.call-start = ((), (), s32[]{:S(2)}) async-start(), calls=%async_computation.14 | async-start | bytes 2228224 | tf_op jit(solution)/shard_map/all_gather | solution.py:45
  744.3 108.3 %all-reduce.27.cloned.1.call-start = ((), (), s32[]{:S(2)}) async-start(), calls=%async_computation.15 | async-start | bytes 262144 | tf_op jit(solution)/shard_map/psum | solution.py:42
  792.5 108.8 %all-gather.27.cloned.1.call-start = ((), (), s32[]{:S(2)}) async-start(), calls=%async_computation.16 | async-start | bytes 2228224 | tf_op jit(solution)/shard_map/all_gather | solution.py:45
  854.4 111.2 %all-reduce.29.cloned.1.call-start = ((), (), s32[]{:S(2)}) async-start(), calls=%async_computation.17 | async-start | bytes 262144 | tf_op jit(solution)/shard_map/psum | solution.py:42
  906.1 108.2 %all-gather.29.cloned.1.call-start = ((), (), s32[]{:S(2)}) async-start(), calls=%async_computation.18 | async-start | bytes 2228224 | tf_op jit(solution)/shard_map/all_gather | solution.py:45
  968.1 108.4 %all-reduce.31.cloned.1.call-start = ((), (), s32[]{:S(2)}) async-start(), calls=%async_computation.19 | async-start | bytes 262144 | tf_op jit(solution)/shard_map/psum | solution.py:42
  1016.2 109.1 %all-gather.31.cloned.1.call-start = ((), (), s32[]{:S(2)}) async-start(), calls=%async_computation.20 | async-start | bytes 2228224 | tf_op jit(solution)/shard_map/all_gather | solution.py:45
  1079.1 108.5 %all-reduce.33.cloned.1.call-start = ((), (), s32[]{:S(2)}) async-start(), calls=%async_computation.21 | async-start | bytes 262144 | tf_op jit(solution)/shard_map/psum | solution.py:42
  1127.3 109.3 %all-gather.33.cloned.1.call-start = ((), (), s32[]{:S(2)}) async-start(), calls=%async_computation.22 | async-start | bytes 2228224 | tf_op jit(solution)/shard_map/all_gather | solution.py:45
  1190.3 108.5 %all-reduce.35.cloned.1.call-start = ((), (), s32[]{:S(2)}) async-start(), calls=%async_computation.23 | async-start | bytes 262144 | tf_op jit(solution)/shard_map/psum | solution.py:42
  1238.5 109.0 %all-gather.35.cloned.1.call-start = ((), (), s32[]{:S(2)}) async-start(), calls=%async_computation.24 | async-start | bytes 2228224 | tf_op jit(solution)/shard_map/all_gather | solution.py:45
  1300.5 87.6 %reduce-scatter.2.cloned.1.call-start = ((), (), s32[]{:S(2)}) async-start(), calls=%async_computation.25 | async-start | bytes 1769472 | tf_op jit(solution)/shard_map/reduce_scatter | solution.py:100
  (14 other events, 1878.5 us)
Sparse Core Ops, SparseCore 0:
  11.0 62.3 all-reduce.12
  76.1 46.0 all-gather.12
  125.1 59.2 all-reduce.14
  187.1 46.0 all-gather.14
  236.0 59.2 all-reduce.16
  298.2 46.0 all-gather.16
  347.2 59.2 all-reduce.18
  409.2 46.0 all-gather.18
  460.2 59.2 all-reduce.20
  522.2 46.0 all-gather.20
  571.2 59.2 all-reduce.22
  633.3 46.0 all-gather.22
  682.3 59.2 all-reduce.24
  744.4 46.0 all-gather.24
  793.3 59.2 all-reduce.26
  855.2 46.0 all-gather.26
  906.2 59.2 all-reduce.28
  968.2 46.0 all-gather.28
  1017.2 59.2 all-reduce.30
  1079.2 46.0 all-gather.30
  1128.3 59.2 all-reduce.32
  1190.4 46.0 all-gather.32
  1239.5 59.2 all-reduce.34
  1301.3 46.0 all-gather.34
  (1 shorter events, 32.2 us)
where the time goes:
time: 1400 us
  waiting for transfers between devices  1300 us (93%)
  other arithmetic  37.5 us (3%)
  matrix products  28.1 us (2%)
  local copies, waits for them, and re-layouts  17.3 us (1%)
  between operations  14.6 us (1%)
    psum x12, waiting for transfers between devices, reduce_rows(): return lax.psum(partial_value, 'col')  723 us
    all_gather x12, waiting for transfers between devices, spread_rows(): return lax.all_gather(values, 'row', axis=0, tiled=True)  544 us
    reduce_scatter x1, waiting for transfers between devices, body(): lax.psum_scatter(fold_pair(jnp.dot(z_flat, picked, preferred_element_type...  31.1 us
  transfers between devices with their start and end apart: 25, of which 25 were waited for; matrix products, arithmetic and copies ran while one was open for 1% of the time, Pallas kernels for 0%

commit v1 on v0

--- a/solution.py
+++ b/solution.py
@@ -4,6 +4,11 @@
 from jax.sharding import PartitionSpec as P
 
 NEUMANN = 3
+
+
+def add_all(value, axis):
+    shards = lax.all_gather(value, axis)
+    return jnp.sum(shards, axis=0)
 
 
 def split_pair(values):
@@ -39,7 +44,7 @@
     local_start = row_idx * row_block
 
     def reduce_rows(partial_value):
-        return lax.psum(partial_value, "col")
+        return add_all(partial_value, "col")
 
     def spread_rows(values):
         return lax.all_gather(values, "row", axis=0, tiled=True)

time: 1400 us -> 964 us (0.69)
  waiting for transfers between devices: 1300 us -> 861 us
  local copies, waits for them, and re-layouts: 17.3 us -> 36.2 us
  other arithmetic: 37.5 us -> 21.3 us
    psum x12 -> x0, waiting for transfers between devices: 723 us -> none  [reduce_rows(): return lax.psum(partial_value, 'col')]
    all_gather x0 -> x12, waiting for transfers between devices: none -> 276 us  [add_all(): shards = lax.all_gather(value, axis)]
    unnamed x32, local copies, waits for them, and re-layouts: 13.9 us -> 32.8 us
  transfers between devices with their start and end apart: 25 -> 25, of which waited for: 25 -> 25; matrix products, arithmetic and copies ran while one was open for 1% -> 2% of each run, Pallas kernels for 0% -> 0%
where the time goes in v1:
time: 964 us; the launch traced here: 962 us
  waiting for transfers between devices  861 us (89%)
  local copies, waits for them, and re-layouts  36.2 us (4%)
  matrix products  28.1 us (3%)
  other arithmetic  21.3 us (2%)
  between operations  14.7 us (2%)
    all_gather x12, waiting for transfers between devices, spread_rows(): return lax.all_gather(values, 'row', axis=0, tiled=True)  553 us
    all_gather x12, waiting for transfers between devices, add_all(): shards = lax.all_gather(value, axis)  276 us
    unnamed x32, local copies, waits for them, and re-layouts  32.8 us
    reduce_scatter x1, waiting for transfers between devices, body(): lax.psum_scatter(fold_pair(jnp.dot(z_flat, picked, preferred_element_type...  31.1 us
  transfers between devices with their start and end apart: 25, of which 25 were waited for; matrix products, arithmetic and copies ran while one was open for 2% of the time, Pallas kernels for 0%

profile of v1, /device:TPU:0, one launch (start us, length us, event | category | flops | bytes accessed | tf_op | source)
XLA Modules:
  0.0 962.5 jit_solution(871236657500039584)
XLA Ops:
  11.0 25.7 %all-gather.61.cloned.1.call-done = f32[2048,128]{0,1:T(8,128)} async-done(((f32[256,128]{0,1:T(8,128)}), f32[2048,128]{0,1:T(8,128)}) %all-gather.61.cloned.1.call-update) | async-done | bytes 1048592 | tf_op jit(solution)/shard_map/all_gather | solution.py:10
  39.4 47.2 %all-gather.37.cloned.1.call-done = bf16[4096,256]{0,1:T(8,128)(2,1)} async-done(((bf16[256,256]{0,1:T(8,128)(2,1)}), bf16[4096,256]{0,1:T(8,128)(2,1)}) %all-gather.37.cloned.1.call-update) | async-done | bytes 2097168 | tf_op jit(solution)/shard_map/all_gather | solution.py:50
  88.6 22.9 %all-gather.63.cloned.1.call-done = f32[2048,128]{0,1:T(8,128)} async-done(((f32[256,128]{0,1:T(8,128)}), f32[2048,128]{0,1:T(8,128)}) %all-gather.63.cloned.1.call-update) | async-done | bytes 1048592 | tf_op jit(solution)/shard_map/all_gather | solution.py:10
  114.1 47.2 %all-gather.39.cloned.1.call-done = bf16[4096,256]{0,1:T(8,128)(2,1)} async-done(((bf16[256,256]{0,1:T(8,128)(2,1)}), bf16[4096,256]{0,1:T(8,128)(2,1)}) %all-gather.39.cloned.1.call-update) | async-done | bytes 2097168 | tf_op jit(solution)/shard_map/all_gather | solution.py:50
  163.3 22.7 %all-gather.65.cloned.1.call-done = f32[2048,128]{0,1:T(8,128)} async-done(((f32[256,128]{0,1:T(8,128)}), f32[2048,128]{0,1:T(8,128)}) %all-gather.65.cloned.1.call-update) | async-done | bytes 1048592 | tf_op jit(solution)/shard_map/all_gather | solution.py:10
  188.7 47.2 %all-gather.41.cloned.1.call-done = bf16[4096,256]{0,1:T(8,128)(2,1)} async-done(((bf16[256,256]{0,1:T(8,128)(2,1)}), bf16[4096,256]{0,1:T(8,128)(2,1)}) %all-gather.41.cloned.1.call-update) | async-done | bytes 2097168 | tf_op jit(solution)/shard_map/all_gather | solution.py:50
  237.9 22.8 %all-gather.67.cloned.1.call-done = f32[2048,128]{0,1:T(8,128)} async-done(((f32[256,128]{0,1:T(8,128)}), f32[2048,128]{0,1:T(8,128)}) %all-gather.67.cloned.1.call-update) | async-done | bytes 1048592 | tf_op jit(solution)/shard_map/all_gather | solution.py:10
  263.5 47.2 %all-gather.43.cloned.1.call-done = bf16[4096,256]{0,1:T(8,128)(2,1)} async-done(((bf16[256,256]{0,1:T(8,128)(2,1)}), bf16[4096,256]{0,1:T(8,128)(2,1)}) %all-gather.43.cloned.1.call-update) | async-done | bytes 2097168 | tf_op jit(solution)/shard_map/all_gather | solution.py:50
  315.7 22.5 %all-gather.69.cloned.1.call-done = f32[2048,128]{0,1:T(8,128)} async-done(((f32[256,128]{0,1:T(8,128)}), f32[2048,128]{0,1:T(8,128)}) %all-gather.69.cloned.1.call-update) | async-done | bytes 1048592 | tf_op jit(solution)/shard_map/all_gather | solution.py:10
  340.8 47.2 %all-gather.45.cloned.1.call-done = bf16[4096,256]{0,1:T(8,128)(2,1)} async-done(((bf16[256,256]{0,1:T(8,128)(2,1)}), bf16[4096,256]{0,1:T(8,128)(2,1)}) %all-gather.45.cloned.1.call-update) | async-done | bytes 2097168 | tf_op jit(solution)/shard_map/all_gather | solution.py:50
  390.0 22.9 %all-gather.71.cloned.1.call-done = f32[2048,128]{0,1:T(8,128)} async-done(((f32[256,128]{0,1:T(8,128)}), f32[2048,128]{0,1:T(8,128)}) %all-gather.71.cloned.1.call-update) | async-done | bytes 1048592 | tf_op jit(solution)/shard_map/all_gather | solution.py:10
  415.5 47.2 %all-gather.47.cloned.1.call-done = bf16[4096,256]{0,1:T(8,128)(2,1)} async-done(((bf16[256,256]{0,1:T(8,128)(2,1)}), bf16[4096,256]{0,1:T(8,128)(2,1)}) %all-gather.47.cloned.1.call-update) | async-done | bytes 2097168 | tf_op jit(solution)/shard_map/all_gather | solution.py:50
  464.6 22.9 %all-gather.73.cloned.1.call-done = f32[2048,128]{0,1:T(8,128)} async-done(((f32[256,128]{0,1:T(8,128)}), f32[2048,128]{0,1:T(8,128)}) %all-gather.73.cloned.1.call-update) | async-done | bytes 1048592 | tf_op jit(solution)/shard_map/all_gather | solution.py:10
  490.3 47.2 %all-gather.49.cloned.1.call-done = bf16[4096,256]{0,1:T(8,128)(2,1)} async-done(((bf16[256,256]{0,1:T(8,128)(2,1)}), bf16[4096,256]{0,1:T(8,128)(2,1)}) %all-gather.49.cloned.1.call-update) | async-done | bytes 2097168 | tf_op jit(solution)/shard_map/all_gather | solution.py:50
  539.4 22.7 %all-gather.75.cloned.1.call-done = f32[2048,128]{0,1:T(8,128)} async-done(((f32[256,128]{0,1:T(8,128)}), f32[2048,128]{0,1:T(8,128)}) %all-gather.75.cloned.1.call-update) | async-done | bytes 1048592 | tf_op jit(solution)/shard_map/all_gather | solution.py:10
  565.1 46.9 %all-gather.51.cloned.1.call-done = bf16[4096,256]{0,1:T(8,128)(2,1)} async-done(((bf16[256,256]{0,1:T(8,128)(2,1)}), bf16[4096,256]{0,1:T(8,128)(2,1)}) %all-gather.51.cloned.1.call-update) | async-done | bytes 2097168 | tf_op jit(solution)/shard_map/all_gather | solution.py:50
  642.1 47.2 %all-gather.53.cloned.1.call-done = bf16[4096,256]{0,1:T(8,128)(2,1)} async-done(((bf16[256,256]{0,1:T(8,128)(2,1)}), bf16[4096,256]{0,1:T(8,128)(2,1)}) %all-gather.53.cloned.1.call-update) | async-done | bytes 2097168 | tf_op jit(solution)/shard_map/all_gather | solution.py:50
  691.3 22.9 %all-gather.79.cloned.1.call-done = f32[2048,128]{0,1:T(8,128)} async-done(((f32[256,128]{0,1:T(8,128)}), f32[2048,128]{0,1:T(8,128)}) %all-gather.79.cloned.1.call-update) | async-done | bytes 1048592 | tf_op jit(solution)/shard_map/all_gather | solution.py:10
  716.8 47.2 %all-gather.55.cloned.1.call-done = bf16[4096,256]{0,1:T(8,128)(2,1)} async-done(((bf16[256,256]{0,1:T(8,128)(2,1)}), bf16[4096,256]{0,1:T(8,128)(2,1)}) %all-gather.55.cloned.1.call-update) | async-done | bytes 2097168 | tf_op jit(solution)/shard_map/all_gather | solution.py:50
  765.9 22.9 %all-gather.81.cloned.1.call-done = f32[2048,128]{0,1:T(8,128)} async-done(((f32[256,128]{0,1:T(8,128)}), f32[2048,128]{0,1:T(8,128)}) %all-gather.81.cloned.1.call-update) | async-done | bytes 1048592 | tf_op jit(solution)/shard_map/all_gather | solution.py:10
  791.5 47.2 %all-gather.57.cloned.1.call-done = bf16[4096,256]{0,1:T(8,128)(2,1)} async-done(((bf16[256,256]{0,1:T(8,128)(2,1)}), bf16[4096,256]{0,1:T(8,128)(2,1)}) %all-gather.57.cloned.1.call-update) | async-done | bytes 2097168 | tf_op jit(solution)/shard_map/all_gather | solution.py:50
  840.7 22.9 %all-gather.83.cloned.1.call-done = f32[2048,128]{0,1:T(8,128)} async-done(((f32[256,128]{0,1:T(8,128)}), f32[2048,128]{0,1:T(8,128)}) %all-gather.83.cloned.1.call-update) | async-done | bytes 1048592 | tf_op jit(solution)/shard_map/all_gather | solution.py:10
  878.9 34.6 %all-gather.59.cloned.1.call-done = bf16[4096,256]{0,1:T(8,128)(2,1)} async-done(((bf16[256,256]{0,1:T(8,128)(2,1)}), bf16[4096,256]{0,1:T(8,128)(2,1)}) %all-gather.59.cloned.1.call-update) | async-done | bytes 2097168 | tf_op jit(solution)/shard_map/all_gather | solution.py:50
  923.0 31.1 %reduce-scatter.2.cloned.1.call-done = f32[384,128]{0,1:T(8,128)} async-done(((f32[3072,128]{0,1:T(8,128)}), f32[384,128]{0,1:T(8,128)}) %reduce-scatter.2.cloned.1.call-update) | async-done | bytes 196624 | tf_op jit(solution)/shard_map/reduce_scatter | solution.py:105
  (176 shorter events, 109.5 us)
Async XLA Ops:
  10.8 75.8 %all-gather.37.cloned.1.call-start = ((), (), s32[]{:S(2)}) async-start(), calls=%async_computation.1 | async-start | bytes 2228224 | tf_op jit(solution)/shard_map/all_gather | solution.py:50
  39.4 72.1 %all-gather.63.cloned.1.call-start = ((), (), s32[]{:S(2)}) async-start(), calls=%async_computation.15 | async-start | bytes 1179648 | tf_op jit(solution)/shard_map/all_gather | solution.py:10
  88.6 72.7 %all-gather.39.cloned.1.call-start = ((), (), s32[]{:S(2)}) async-start(), calls=%async_computation.2 | async-start | bytes 2228224 | tf_op jit(solution)/shard_map/all_gather | solution.py:50
  114.0 71.9 %all-gather.65.cloned.1.call-start = ((), (), s32[]{:S(2)}) async-start(), calls=%async_computation.16 | async-start | bytes 1179648 | tf_op jit(solution)/shard_map/all_gather | solution.py:10
  163.2 72.7 %all-gather.41.cloned.1.call-start = ((), (), s32[]{:S(2)}) async-start(), calls=%async_computation.3 | async-start | bytes 2228224 | tf_op jit(solution)/shard_map/all_gather | solution.py:50
  188.7 72.1 %all-gather.67.cloned.1.call-start = ((), (), s32[]{:S(2)}) async-start(), calls=%async_computation.17 | async-start | bytes 1179648 | tf_op jit(solution)/shard_map/all_gather | solution.py:10
  237.8 72.9 %all-gather.43.cloned.1.call-start = ((), (), s32[]{:S(2)}) async-start(), calls=%async_computation.4 | async-start | bytes 2228224 | tf_op jit(solution)/shard_map/all_gather | solution.py:50
  263.5 74.7 %all-gather.69.cloned.1.call-start = ((), (), s32[]{:S(2)}) async-start(), calls=%async_computation.18 | async-start | bytes 1179648 | tf_op jit(solution)/shard_map/all_gather | solution.py:10
  315.5 72.5 %all-gather.45.cloned.1.call-start = ((), (), s32[]{:S(2)}) async-start(), calls=%async_computation.5 | async-start | bytes 2228224 | tf_op jit(solution)/shard_map/all_gather | solution.py:50
  340.8 72.1 %all-gather.71.cloned.1.call-start = ((), (), s32[]{:S(2)}) async-start(), calls=%async_computation.19 | async-start | bytes 1179648 | tf_op jit(solution)/shard_map/all_gather | solution.py:10
  389.9 72.7 %all-gather.47.cloned.1.call-start = ((), (), s32[]{:S(2)}) async-start(), calls=%async_computation.6 | async-start | bytes 2228224 | tf_op jit(solution)/shard_map/all_gather | solution.py:50
  415.4 72.1 %all-gather.73.cloned.1.call-start = ((), (), s32[]{:S(2)}) async-start(), calls=%async_computation.20 | async-start | bytes 1179648 | tf_op jit(solution)/shard_map/all_gather | solution.py:10
  464.6 72.9 %all-gather.49.cloned.1.call-start = ((), (), s32[]{:S(2)}) async-start(), calls=%async_computation.7 | async-start | bytes 2228224 | tf_op jit(solution)/shard_map/all_gather | solution.py:50
  490.2 71.9 %all-gather.75.cloned.1.call-start = ((), (), s32[]{:S(2)}) async-start(), calls=%async_computation.21 | async-start | bytes 1179648 | tf_op jit(solution)/shard_map/all_gather | solution.py:10
  539.4 72.7 %all-gather.51.cloned.1.call-start = ((), (), s32[]{:S(2)}) async-start(), calls=%async_computation.8 | async-start | bytes 2228224 | tf_op jit(solution)/shard_map/all_gather | solution.py:50
  564.8 74.7 %all-gather.77.cloned.1.call-start = ((), (), s32[]{:S(2)}) async-start(), calls=%async_computation.22 | async-start | bytes 1179648 | tf_op jit(solution)/shard_map/all_gather | solution.py:10
  616.8 72.5 %all-gather.53.cloned.1.call-start = ((), (), s32[]{:S(2)}) async-start(), calls=%async_computation.9 | async-start | bytes 2228224 | tf_op jit(solution)/shard_map/all_gather | solution.py:50
  642.1 72.1 %all-gather.79.cloned.1.call-start = ((), (), s32[]{:S(2)}) async-start(), calls=%async_computation.23 | async-start | bytes 1179648 | tf_op jit(solution)/shard_map/all_gather | solution.py:10
  691.2 72.7 %all-gather.55.cloned.1.call-start = ((), (), s32[]{:S(2)}) async-start(), calls=%async_computation.10 | async-start | bytes 2228224 | tf_op jit(solution)/shard_map/all_gather | solution.py:50
  716.7 72.1 %all-gather.81.cloned.1.call-start = ((), (), s32[]{:S(2)}) async-start(), calls=%async_computation.24 | async-start | bytes 1179648 | tf_op jit(solution)/shard_map/all_gather | solution.py:10
  765.9 72.9 %all-gather.57.cloned.1.call-start = ((), (), s32[]{:S(2)}) async-start(), calls=%async_computation.11 | async-start | bytes 2228224 | tf_op jit(solution)/shard_map/all_gather | solution.py:50
  791.5 72.1 %all-gather.83.cloned.1.call-start = ((), (), s32[]{:S(2)}) async-start(), calls=%async_computation.25 | async-start | bytes 1179648 | tf_op jit(solution)/shard_map/all_gather | solution.py:10
  840.7 72.8 %all-gather.59.cloned.1.call-start = ((), (), s32[]{:S(2)}) async-start(), calls=%async_computation.12 | async-start | bytes 2228224 | tf_op jit(solution)/shard_map/all_gather | solution.py:50
  866.2 87.9 %reduce-scatter.2.cloned.1.call-start = ((), (), s32[]{:S(2)}) async-start(), calls=%async_computation.13 | async-start | bytes 1769472 | tf_op jit(solution)/shard_map/reduce_scatter | solution.py:105
  (8 other events, 221.9 us)
Sparse Core Ops, SparseCore 0:
  10.9 25.7 all-gather.60
  39.5 47.0 all-gather.36
  88.9 22.5 all-gather.62
  114.2 47.0 all-gather.38
  163.4 22.5 all-gather.64
  188.8 47.0 all-gather.40
  238.2 22.5 all-gather.66
  263.6 47.0 all-gather.42
  315.6 22.5 all-gather.68
  340.9 47.0 all-gather.44
  390.3 22.5 all-gather.70
  415.5 47.0 all-gather.46
  464.9 22.5 all-gather.72
  490.3 47.0 all-gather.48
  539.6 22.5 all-gather.74
  564.9 47.0 all-gather.50
  642.2 47.0 all-gather.52
  691.6 22.5 all-gather.78
  716.8 47.0 all-gather.54
  766.2 22.5 all-gather.80
  791.6 47.0 all-gather.56
  841.0 22.5 all-gather.82
  866.4 47.0 all-gather.58
  921.9 32.2 reduce-scatter.1
  (1 shorter events, 22.5 us)
